TPU v7x, 32 devices: a whole 2x2x4 slice. The times are simulated.
32 devices in a mesh: chol: 8 (over z, x), orb: 4 (over y, core).
Axes of the slice: x: 2, y: 2, z: 4, core: 2. Of those that a mesh axis runs over, the one named last changes fastest.
Arguments:
- b_vectors: bfloat16 [16, 6400, 6400], P('chol', 'orb'), as said below
- gamma_density: bfloat16 [16, 6400, 400], P('chol', 'orb'), may hold values from -2 to 2
Outputs:
- orbital_gradient: float32 [6400, 400], P('orb', 'chol')
Inputs may be any that keep to these rules, and one draw needn't show every extreme that they name: Each b_vectors[Q] is a symmetric matrix.
All inputs are finite; a program needn't handle non-finite values.
Results may differ from a plain program's by a relative error of at most 0.0003.
Values may be sent and summed in bfloat16 or wider, within the bound.
A program may use at most 128 MiB of HBM per device.

v0:
```python
import jax
import jax.numpy as jnp
from jax import lax
from jax.sharding import PartitionSpec as P

NMO = 6400
NOCC = 400


def shards(b_vectors, gamma_density):
    partial_sum = jnp.einsum(
        "qpr,qri->pi",
        b_vectors,
        lax.all_gather(gamma_density, "orb", axis=1, tiled=True),
        preferred_element_type=jnp.float32,
    )
    row_block = lax.psum_scatter(partial_sum, "chol", scatter_dimension=1, tiled=True)
    stride = NMO // NOCC
    own_occupied = row_block[::stride]
    full_columns = lax.all_gather(own_occupied, "chol", axis=1, tiled=True)
    exchanged = lax.all_to_all(full_columns, "orb", split_axis=1, concat_axis=0, tiled=True)
    flipped = exchanged.T
    col_offset = lax.axis_index("chol") * row_block.shape[1]
    mirrored = lax.dynamic_slice_in_dim(flipped, col_offset, row_block.shape[1], 1)
    return row_block.at[::stride].set(own_occupied - mirrored)


def solution(mesh):
    in_specs = (P("chol", "orb", None), P("chol", "orb", None))
    out_specs = P("orb", "chol")
    return jax.shard_map(shards, mesh=mesh, in_specs=in_specs, out_specs=out_specs, check_vma=False)
```

profile of v0, /device:TPU:0, one launch (start us, length us, event | category | flops | bytes accessed | tf_op | source)
XLA Modules:
  0.0 273.5 jit_solution(17193519250920760950)
XLA Ops:
  6.5 0.0 all-gather.3.cloned.1.call-start
  6.5 9.1 %copy.7 = bf16[2,1600,400]{2,0,1:T(2,128)(2,1)} copy(bf16[2,1600,400]{1,2,0:T(8,128)(2,1)} %param.3) | data formatting | bytes 5120000 | tf_op args[1]
  15.7 0.0 all-gather.3.cloned.1.call-update
  15.7 0.0 copy-start
  15.7 87.9 %all-gather.3.cloned.1.call-done = bf16[2,6400,400]{2,0,1:T(2,128)(2,1)} async-done(((bf16[2,1600,400]{2,0,1:T(2,128)(2,1)}), bf16[2,6400,400]{2,0,1:T(2,128)(2,1)}) %all-gather.3.cloned.1.call-update) | async-done | bytes 10240016 | tf_op jit(solution)/shard_map/all_gather | solution.py:14
  103.6 26.5 %fusion.3 = f32[1600,400]{0,1:T(8,128)S(1)} fusion(bf16[2,1600,6400]{2,1,0:T(8,128)(2,1)} %param.2, bf16[2,6400,400]{2,0,1:T(2,128)(2,1)} %all-gather.3.cloned.1.call-done), kind=kOutput, calls=%fused_computation.3 | convolution fusion | flops 16384000000 | bytes 53760000 | tf_op jit(solution)/shard_map/qpr,qri->pi/dot_general | solution.py:11
  130.1 73.3 %fusion = f32[1600,64]{0,1:T(8,128)S(1)} fusion(f32[1600,400]{0,1:T(8,128)S(1)} %fusion.3), kind=kCustom, calls=%all-reduce-scatter | all-reduce-scatter fusion | flops 819201 | bytes 2970112
  203.4 4.4 %collective-permute-start = (f32[1600,64]{0,1:T(8,128)S(1)}, f32[1600,64]{0,1:T(8,128)S(1)}, u32[]{:S(2)}, u32[]{:S(2)}) collective-permute-start(f32[1600,64]{0,1:T(8,128)S(1)} %fusion), channel_id=1, source_target_pairs={{0,4},{4,8},{8,12},{12,16},{16,20},{20,24},{24,28},{1,5},{5,9},{9,... | collective-permute-start | bytes 1228808
  207.8 1.3 collective-permute-start.1
  209.1 0.0 copy-done
  209.1 0.6 dynamic-slice.8
  210.4 2.7 collective-permute-done.1
  213.0 0.4 collective-permute-done
  213.4 0.8 concatenate
  214.2 0.8 slice.3
  215.1 39.6 %all-gather = f32[8,50,100]{2,1,0:T(8,128)S(1)} all-gather(f32[1,50,100]{2,1,0:T(8,128)S(1)} %bitcast.19), channel_id=1, replica_groups=mesh['chol'=8,'orb'=4] {'chol'}, dimensions={0}, use_global_device_ids=true | all-gather | bytes 180000 | tf_op jit(solution)/shard_map/all_gather | solution.py:20
  254.7 0.7 all_to_all.14
  255.4 3.4 %all-to-all-start = ((f32[100,4,100]{0,2,1:T(8,128)}), f32[100,4,100]{0,2,1:T(8,128)S(1)}, u32[]{:S(2)}, u32[]{:S(2)}) async-start(f32[100,4,100]{0,2,1:T(8,128)} %all_to_all.14), calls=%async_computation | async-start | bytes 425984 | tf_op jit(solution)/shard_map/all_to_all | solution.py:21
  258.8 0.3 copy.10
  259.1 5.1 %all-to-all-done = f32[100,4,100]{0,2,1:T(8,128)S(1)} async-done(((f32[100,4,100]{0,2,1:T(8,128)}), f32[100,4,100]{0,2,1:T(8,128)S(1)}, u32[]{:S(2)}, u32[]{:S(2)}) %all-to-all-start) | async-done | bytes 160032 | tf_op jit(solution)/shard_map/all_to_all | solution.py:21
  264.2 0.1 copy.9
  264.4 0.1 copy.11
  264.5 1.1 scatter_fusion
  265.6 1.0 copy.12
  (6 shorter events, 0.1 us)
Async XLA Ops:
  6.5 97.1 %all-gather.3.cloned.1.call-start = ((), (), s32[]{:S(2)}) async-start(), calls=%async_computation.1 | async-start | bytes 16384000 | tf_op jit(solution)/shard_map/all_gather | solution.py:14
  15.7 193.4 %copy-start = (u32[32]{0:T(128)S(1)}, u32[32]{0:T(128)}, u32[]{:S(2)}) copy-start(u32[32]{0:T(128)} %constant.18) | copy-start | bytes 388
  203.4 10.0 %collective-permute-start = (f32[1600,64]{0,1:T(8,128)S(1)}, f32[1600,64]{0,1:T(8,128)S(1)}, u32[]{:S(2)}, u32[]{:S(2)}) collective-permute-start(f32[1600,64]{0,1:T(8,128)S(1)} %fusion), channel_id=1, source_target_pairs={{0,4},{4,8},{8,12},{12,16},{16,20},{20,24},{24,28},{1,5},{5,9},{9,... | collective-permute-start | bytes 1228808
  207.8 5.2 %collective-permute-start.1 = (f32[1600,34]{0,1:T(8,128)S(1)}, f32[1600,34]{0,1:T(8,128)S(1)}, u32[]{:S(2)}, u32[]{:S(2)}) collective-permute-start(f32[1600,34]{0,1:T(8,128)S(1)} %slice.4), channel_id=1, source_target_pairs={{0,8},{4,12},{8,16},{12,20},{16,24},{20,28},{1,9},{5,13},{9,17},{1... | collective-permute-start | bytes 652808
  255.4 8.8 %all-to-all-start = ((f32[100,4,100]{0,2,1:T(8,128)}), f32[100,4,100]{0,2,1:T(8,128)S(1)}, u32[]{:S(2)}, u32[]{:S(2)}) async-start(f32[100,4,100]{0,2,1:T(8,128)} %all_to_all.14), calls=%async_computation | async-start | bytes 425984 | tf_op jit(solution)/shard_map/all_to_all | solution.py:21
Sparse Core Ops, SparseCore 0:
  15.8 87.7 all-gather.2
where the time goes:
time: 274 us
  blocking collectives  113 us (41%)
  waiting for transfers between devices  96.1 us (35%)
  matrix products  26.5 us (10%)
  local copies, waits for them, and re-layouts  14.9 us (5%)
  between operations  14.2 us (5%)
  starting transfers between devices  9.09 us (3%)
    all_gather x1, waiting for transfers between devices, shards(): lax.all_gather(gamma_density, 'orb', axis=1, tiled=True)  87.9 us
    unnamed x1, blocking collectives  73.3 us
    all_gather x1, blocking collectives, shards(): full_columns = lax.all_gather(own_occupied, 'chol', axis=1, tiled=True)  39.6 us
    dot_general x1, matrix products, shards(): jnp.einsum('qpr,qri->pi', b_vectors, lax.all_gather(gamma_density, 'orb',...  26.5 us
    unnamed x8, local copies, waits for them, and re-layouts  10.6 us
    unnamed x2, starting transfers between devices  5.71 us
  transfers between devices with their start and end apart: 4, of which 4 were waited for; matrix products, arithmetic and copies ran while one was open for 0% of the time, Pallas kernels for 0%

commit v1 on v0

v1 whole, which is shorter than its diff:
```python
import functools

import jax
import jax.numpy as jnp
from jax import lax
from jax.experimental import pallas as pl
from jax.experimental.pallas import tpu as pltpu
from jax.sharding import PartitionSpec as P

LANES = 128
PAIR = 2
LAG1, LAG2, LAG3 = 1, 3, 5
MESH = pl.DeviceIdType.MESH
F32 = jnp.float32


def gathered(b_vectors, gamma_density):
    partial_sum = jnp.einsum(
        "qpr,qri->pi",
        b_vectors,
        lax.all_gather(gamma_density, "orb", axis=1, tiled=True),
        preferred_element_type=F32,
    )
    row_block = lax.psum_scatter(partial_sum, "chol", scatter_dimension=1, tiled=True)
    stride = b_vectors.shape[2] // gamma_density.shape[2]
    own_occupied = row_block[::stride]
    full_columns = lax.all_gather(own_occupied, "chol", axis=1, tiled=True)
    exchanged = lax.all_to_all(full_columns, "orb", split_axis=1, concat_axis=0, tiled=True)
    flipped = exchanged.T
    col_offset = lax.axis_index("chol") * row_block.shape[1]
    mirrored = lax.dynamic_slice_in_dim(flipped, col_offset, row_block.shape[1], 1)
    return row_block.at[::stride].set(own_occupied - mirrored)


def kernel(nz, rows, cols, stride, ha,
           b_ref, g_ref, out_ref,
           bbuf, gt, cbuf, rc, s, rx1, ry1, rx2, ry2, zown, zr, zl, f, ms, mr,
           bsem, csem, x1sem, y1sem, x2sem, y2sem, rsem, lsem, msem):
    c, o = lax.axis_index("chol"), lax.axis_index("orb")
    z, x = c // PAIR, lax.rem(c, PAIR)
    y, k = o // PAIR, lax.rem(o, PAIR)
    depth = g_ref.shape[0]
    nvec = b_ref.shape[0]
    nocc = g_ref.shape[1]
    hx = nocc // PAIR
    half = PAIR * rows
    nch = s.shape[0]
    shift = half // LANES - nch
    zrows = zown.shape[2]

    core_id = (c, o + 1 - 2 * k)
    x_id = (c + 1 - 2 * x, o)
    y_id = (c, o + PAIR - 2 * PAIR * y)
    right_id = (c + PAIR, o)
    left_id = (c - PAIR, o)

    def fetches(j, side):
        quadrant = 1 - k if side == 0 else k
        slot = PAIR * lax.rem(j, 2) + side
        out = []
        for q in range(nvec):
            for yy in range(PAIR):
                lane = pl.multiple_of((yy * (half // LANES) + quadrant * shift + j) * LANES, LANES)
                out.append(pltpu.make_async_copy(
                    b_ref.at[q, :, pl.ds(lane, LANES)],
                    bbuf.at[slot, q * rows:(q + 1) * rows, yy * LANES:(yy + 1) * LANES],
                    bsem.at[slot, q * PAIR + yy]))
        return out

    def remote(src, dst, sems, j, target):
        return pltpu.make_async_remote_copy(
            src_ref=src, dst_ref=dst, send_sem=sems.at[0, j], recv_sem=sems.at[1, j],
            device_id=target, device_id_type=MESH)

    def core_copy(j):
        return remote(cbuf.at[j], rc.at[j], csem, j, core_id)

    def x1_copy(j):
        return remote(s.at[j, :, 1 - x, 0:ha], rx1.at[j], x1sem, j, x_id)

    def y1_copy(j):
        return remote(s.at[j, 1 - y, :, ha:hx], ry1.at[j], y1sem, j, y_id)

    def y2_copy(j):
        return remote(s.at[j, 1 - y, x, 0:ha], ry2.at[j], y2sem, j, y_id)

    def x2_copy(j):
        return remote(s.at[j, y, 1 - x, ha:hx], rx2.at[j], x2sem, j, x_id)

    def right_copy(j, first):
        return remote(zown.at[j, first:nz], zr.at[j, first:nz], rsem, j, right_id)

    def left_copy(j, last):
        return remote(zown.at[j, 0:last], zl.at[j, 0:last], lsem, j, left_id)

    for j in range(2):
        for side in range(2):
            for copy in fetches(j, side):
                copy.start()

    barrier = pltpu.get_barrier_semaphore()

    def greet(target):
        pl.semaphore_signal(barrier, inc=1, device_id=target, device_id_type=MESH)

    for target in (core_id, x_id, y_id):
        greet(target)

    @pl.when(z > 0)
    def _():
        greet(left_id)

    @pl.when(z < nz - 1)
    def _():
        greet(right_id)

    for h in range(2):
        @pl.when(2 * o + h != c)
        def _():
            greet((2 * o + h, c // 2))

    col = lax.broadcasted_iota(jnp.int32, (nocc, nocc), 1)
    row = lax.broadcasted_iota(jnp.int32, (nocc, nocc), 0)
    origin = row
    for xx in range(PAIR):
        for zz in range(nz):
            start = xx * hx + zz * cols
            delta = (zz * PAIR + xx) * cols - start
            origin = jnp.where((row >= start) & (row < start + cols), row + delta, origin)
    pick = jnp.where(col == origin, 1.0, 0.0).astype(jnp.bfloat16)
    per = max(n for n in range(1, 6) if (depth // LANES) % n == 0) * LANES
    for at in range(0, depth, per):
        gt[:, at:at + per] = lax.dot_general(
            pick, g_ref[at:at + per, :], (((1,), (1,)), ((), ())),
            preferred_element_type=F32).astype(jnp.bfloat16)

    count = 3 + jnp.where(z > 0, 1, 0) + jnp.where(z < nz - 1, 1, 0) + jnp.where(c // 2 == o, 1, 2)
    pl.semaphore_wait(barrier, count)

    def product(t, side):
        slot = PAIR * lax.rem(t, 2) + side
        for copy in fetches(t, side):
            copy.wait()
        dst = cbuf if side == 0 else s
        res = jnp.dot(gt[...], bbuf[slot], preferred_element_type=F32)
        for yy in range(PAIR):
            for xx in range(PAIR):
                dst[t, yy, xx] = res[xx * hx:(xx + 1) * hx, yy * LANES:(yy + 1) * LANES]

        @pl.when(t + 2 < nch)
        def _():
            for copy in fetches(t + 2, side):
                copy.start()

    def at_lag(t, lag, run):
        j = t - lag

        @pl.when((j >= 0) & (j < nch))
        def _():
            run(j)

    def between_cores(j):
        core_copy(j).wait_recv()
        s[j] = s[j] + rc[j]
        x1_copy(j).start()
        y1_copy(j).start()

    def first_done(j):
        x1_copy(j).wait_recv()
        for yy in range(PAIR):
            s[j, yy, x, 0:ha] = s[j, yy, x, 0:ha] + rx1[j, yy]
        y2_copy(j).start()
        y1_copy(j).wait_recv()
        for xx in range(PAIR):
            s[j, y, xx, ha:hx] = s[j, y, xx, ha:hx] + ry1[j, xx]
        x2_copy(j).start()

    def second_done(j):
        y2_copy(j).wait_recv()
        x2_copy(j).wait_recv()
        top = s[j, y, x, 0:ha] + ry2[j]
        bottom = s[j, y, x, ha:hx] + rx2[j]
        whole = jnp.concatenate([top, bottom, jnp.zeros((8, LANES), F32)], axis=0)
        for zz in range(nz):
            zown[j, zz] = whole[zz * cols:zz * cols + zrows]

    def hop(h, j):
        @pl.when(z == h)
        def _():
            if h > 0:
                right_copy(j, h).wait_recv()
                for d in range(h + 1, nz):
                    zown[j, d] = zown[j, d] + zr[j, d]
            if h < nz - 1:
                right_copy(j, h + 1).start()

        m = nz - 1 - h

        @pl.when(z == m)
        def _():
            if h > 0:
                left_copy(j, m + 1).wait_recv()
                for d in range(m):
                    zown[j, d] = zown[j, d] + zl[j, d]
            if m > 0:
                left_copy(j, m).start()

    def collect(j):
        for h in range(nz):
            @pl.when(z == h)
            def _():
                total = zown[j, h]
                if h > 0:
                    total = total + zr[j, h]
                if h < nz - 1:
                    total = total + zl[j, h]
                square = jnp.concatenate([total, jnp.zeros((LANES - zrows, LANES), F32)], axis=0)
                f[pl.ds(pl.multiple_of(j * LANES, LANES), LANES), :] = square.T

    def step(t, carry):
        @pl.when(t < nch)
        def _():
            product(t, 0)
            core_copy(t).start()

        at_lag(t, LAG1, between_cores)
        at_lag(t, LAG2, first_done)
        at_lag(t, LAG3, second_done)
        for h in range(nz):
            at_lag(t, LAG3 + h, functools.partial(hop, h))
        at_lag(t, LAG3 + nz - 1, collect)

        @pl.when(t < nch)
        def _():
            product(t, 1)

        return carry

    lax.fori_loop(0, nch + LAG3 + nz - 1, step, 0)

    off = k * (rows - shift * LANES)

    def mirror_copy(h, slot):
        return pltpu.make_async_remote_copy(
            src_ref=ms.at[h], dst_ref=mr.at[slot], send_sem=msem.at[0, h], recv_sem=msem.at[1, slot],
            device_id=(2 * o + h, c // 2), device_id_type=MESH)

    for h in range(2):
        block = f[pl.ds(off + h * stride * cols, cols, stride), :]
        ms[h] = jnp.concatenate([block, jnp.zeros((zrows - cols, LANES), F32)], axis=0)

        @pl.when(2 * o + h != c)
        def _():
            mirror_copy(h, x).start()

        @pl.when(2 * o + h == c)
        def _():
            mr[x] = ms[h]

    def drain(j, carry):
        for copy in (core_copy, x1_copy, y1_copy, x2_copy, y2_copy):
            copy(j).wait_send()
        for h in range(nz):
            @pl.when(z == h)
            def _():
                if h < nz - 1:
                    right_copy(j, h + 1).wait_send()
                if h > 0:
                    left_copy(j, h).wait_send()
        return carry

    lax.fori_loop(0, nch, drain, 0)

    for h in range(2):
        @pl.when(2 * o + h != c)
        def _():
            mirror_copy(h, x).wait_send()
            mirror_copy(h, h).wait_recv()

    for h in range(2):
        square = jnp.concatenate([mr[h], jnp.zeros((LANES - zrows, LANES), F32)], axis=0).T
        where = pl.ds(off + h * stride * cols, cols, stride)
        f[where, :] = f[where, :] - square[0:cols]
    out_ref[...] = f[pl.ds(pl.multiple_of(off, 8), rows), 0:cols]


def mirrored_sums(nz, b_vectors, gamma_density):
    nvec, rows, nmo = b_vectors.shape
    nocc = gamma_density.shape[2]
    cols = nocc // (nz * PAIR)
    hx = nocc // PAIR
    ha = (hx // 2 + 7) // 8 * 8
    zrows = (cols + 7) // 8 * 8
    nch = pl.cdiv(rows, LANES)
    depth = nvec * rows
    vmem = pltpu.VMEM
    dma = pltpu.SemaphoreType.DMA
    flops = 2 * depth * nmo * nocc
    return pl.pallas_call(
        functools.partial(kernel, nz, rows, cols, nmo // nocc, ha),
        out_shape=jax.ShapeDtypeStruct((rows, cols), F32),
        in_specs=[pl.BlockSpec(memory_space=pl.ANY), pl.BlockSpec(memory_space=vmem)],
        out_specs=pl.BlockSpec(memory_space=vmem),
        scratch_shapes=[
            vmem((2 * PAIR, depth, PAIR * LANES), jnp.bfloat16),
            vmem((nocc, depth), jnp.bfloat16),
            vmem((nch, PAIR, PAIR, hx, LANES), F32),
            vmem((nch, PAIR, PAIR, hx, LANES), F32),
            vmem((nch, PAIR, PAIR, hx, LANES), F32),
            vmem((nch, PAIR, ha, LANES), F32),
            vmem((nch, PAIR, hx - ha, LANES), F32),
            vmem((nch, hx - ha, LANES), F32),
            vmem((nch, ha, LANES), F32),
            vmem((nch, nz, zrows, LANES), F32),
            vmem((nch, nz, zrows, LANES), F32),
            vmem((nch, nz, zrows, LANES), F32),
            vmem((nch * LANES, LANES), F32),
            vmem((2, zrows, LANES), F32),
            vmem((2, zrows, LANES), F32),
            dma((2 * PAIR, nvec * PAIR)),
            dma((2, nch)),
            dma((2, nch)),
            dma((2, nch)),
            dma((2, nch)),
            dma((2, nch)),
            dma((2, nch)),
            dma((2, nch)),
            dma((2, 2)),
        ],
        compiler_params=pltpu.CompilerParams(
            collective_id=0, has_side_effects=True, vmem_limit_bytes=60 * 2**20
        ),
        cost_estimate=pl.CostEstimate(flops=flops, bytes_accessed=2 * depth * nmo, transcendentals=0),
    )(b_vectors, gamma_density.reshape(depth, nocc))


def solution(mesh):
    nchol, norb = mesh.shape["chol"], mesh.shape["orb"]

    def shards(b_vectors, gamma_density):
        nvec, rows, nmo = b_vectors.shape
        nocc = gamma_density.shape[2]
        fits = (
            norb == PAIR * PAIR
            and nchol == PAIR * norb
            and (PAIR * rows) % LANES == 0
            and rows % 16 == 0
            and nocc % (PAIR * nchol) == 0
            and (nocc // PAIR) % 8 == 0
            and (nvec * rows) % LANES == 0
            and nmo % nocc == 0
            and rows % (nmo // nocc) == 0
        )
        if fits:
            return mirrored_sums(nchol // PAIR, b_vectors, gamma_density)
        return gathered(b_vectors, gamma_density)

    in_specs = (P("chol", "orb", None), P("chol", "orb", None))
    out_specs = P("orb", "chol")
    return jax.shard_map(shards, mesh=mesh, in_specs=in_specs, out_specs=out_specs, check_vma=False)
```

time: 274 us -> 80.8 us (0.29)
  blocking collectives: 113 us -> 0 us
  waiting for transfers between devices: 96.1 us -> 0 us
  Pallas kernels: 0 us -> 72.9 us
  matrix products: 26.5 us -> 0 us
  between operations: 14.2 us -> 0.01 us
  starting transfers between devices: 9.09 us -> 0 us
  local copies, waits for them, and re-layouts: 14.9 us -> 7.44 us
    all_gather x1 -> x0, waiting for transfers between devices: 87.9 us -> none  [shards(): lax.all_gather(gamma_density, 'orb', axis=1, tiled=True)]
    unnamed x1 -> x0, blocking collectives: 73.3 us -> none
    pallas_call x0 -> x1, Pallas kernels: none -> 72.9 us  [mirrored_sums(): pl.pallas_call(functools.partial(kernel, nz, rows, cols, nmo // nocc, ha)...]
    all_gather x1 -> x0, blocking collectives: 39.6 us -> none  [shards(): full_columns = lax.all_gather(own_occupied, 'chol', axis=1, tiled=True)]
    dot_general x1 -> x0, matrix products: 26.5 us -> none  [shards(): jnp.einsum('qpr,qri->pi', b_vectors, lax.all_gather(gamma_density, 'orb',...]
    unnamed x2 -> x0, starting transfers between devices: 5.71 us -> none
    unnamed x8 -> x1, local copies, waits for them, and re-layouts: 10.6 us -> 5.26 us
    all_to_all x1 -> x0, waiting for transfers between devices: 5.12 us -> none  [shards(): lax.all_to_all(full_columns, 'orb', split_axis=1, concat_axis=0, tiled=True)]
  transfers between devices with their start and end apart: 4 -> 0, of which waited for: 4 -> 0; matrix products, arithmetic and copies ran while one was open for 0% -> 0% of each run, Pallas kernels for 0% -> 0%
where the time goes in v1:
time: 80.8 us; the launch traced here: 80.3 us
  Pallas kernels  72.9 us (90%)
  local copies, waits for them, and re-layouts  7.44 us (9%)
    pallas_call x1, Pallas kernels, mirrored_sums(): pl.pallas_call(functools.partial(kernel, nz, rows, cols, nmo // nocc, ha)...  72.9 us
    unnamed x1, local copies, waits for them, and re-layouts  5.26 us
    pallas_call x1, local copies, waits for them, and re-layouts, mirrored_sums(): pl.pallas_call(functools.partial(kernel, nz, rows, cols, nmo // nocc, ha)...  2.19 us

profile of v1, /device:TPU:0, one launch (start us, length us, event | category | flops | bytes accessed | tf_op | source)
XLA Modules:
  0.0 80.3 jit_solution(11627560515883775013)
XLA Ops:
  0.0 5.3 %copy.3 = bf16[2,1600,400]{2,1,0:T(8,128)(2,1)} copy(bf16[2,1600,400]{1,2,0:T(8,128)(2,1)} %param.3) | data formatting | bytes 5120000 | tf_op args[1]
  5.3 72.9 %shard_map.28 = f32[1600,50]{1,0:T(8,128)} custom-call(bf16[2,1600,6400]{2,1,0:T(8,128)(2,1)} %b_ref.1, bf16[3200,400]{1,0:T(8,128)(2,1)} %bitcast.1), custom_call_target="tpu_custom_call" | custom-call | flops 16384000000 | bytes 40960000 | tf_op jit(solution)/shard_map/pallas_call | solution.py:299
  78.1 2.2 %copy.4 = f32[1600,50]{0,1:T(8,128)} copy(f32[1600,50]{1,0:T(8,128)} %shard_map.28) | data formatting | bytes 640000 | tf_op jit(solution)/shard_map/pallas_call | solution.py:299

commit v2 on v1

--- a/solution.py
+++ b/solution.py
@@ -9,7 +9,7 @@
 
 LANES = 128
 PAIR = 2
-LAG1, LAG2, LAG3 = 1, 3, 5
+LAG1, LAG2, LAG3, HOP = 1, 3, 5, 2
 MESH = pl.DeviceIdType.MESH
 F32 = jnp.float32
 
@@ -39,7 +39,6 @@
     c, o = lax.axis_index("chol"), lax.axis_index("orb")
     z, x = c // PAIR, lax.rem(c, PAIR)
     y, k = o // PAIR, lax.rem(o, PAIR)
-    depth = g_ref.shape[0]
     nvec = b_ref.shape[0]
     nocc = g_ref.shape[1]
     hx = nocc // PAIR
@@ -128,11 +127,8 @@
             delta = (zz * PAIR + xx) * cols - start
             origin = jnp.where((row >= start) & (row < start + cols), row + delta, origin)
     pick = jnp.where(col == origin, 1.0, 0.0).astype(jnp.bfloat16)
-    per = max(n for n in range(1, 6) if (depth // LANES) % n == 0) * LANES
-    for at in range(0, depth, per):
-        gt[:, at:at + per] = lax.dot_general(
-            pick, g_ref[at:at + per, :], (((1,), (1,)), ((), ())),
-            preferred_element_type=F32).astype(jnp.bfloat16)
+    parts = [jnp.dot(pick, g_ref[q], preferred_element_type=F32) for q in range(nvec)]
+    gt[...] = jnp.concatenate(parts, axis=1).astype(jnp.bfloat16)
 
     count = 3 + jnp.where(z > 0, 1, 0) + jnp.where(z < nz - 1, 1, 0) + jnp.where(c // 2 == o, 1, 2)
     pl.semaphore_wait(barrier, count)
@@ -227,8 +223,8 @@
         at_lag(t, LAG2, first_done)
         at_lag(t, LAG3, second_done)
         for h in range(nz):
-            at_lag(t, LAG3 + h, functools.partial(hop, h))
-        at_lag(t, LAG3 + nz - 1, collect)
+            at_lag(t, LAG3 + HOP * h, functools.partial(hop, h))
+        at_lag(t, LAG3 + HOP * (nz - 1), collect)
 
         @pl.when(t < nch)
         def _():
@@ -236,7 +232,7 @@
 
         return carry
 
-    lax.fori_loop(0, nch + LAG3 + nz - 1, step, 0)
+    lax.fori_loop(0, nch + LAG3 + HOP * (nz - 1), step, 0)
 
     off = k * (rows - shift * LANES)
 
@@ -331,7 +327,7 @@
             collective_id=0, has_side_effects=True, vmem_limit_bytes=60 * 2**20
         ),
         cost_estimate=pl.CostEstimate(flops=flops, bytes_accessed=2 * depth * nmo, transcendentals=0),
-    )(b_vectors, gamma_density.reshape(depth, nocc))
+    )(b_vectors, jnp.transpose(gamma_density, (0, 2, 1)))
 
 
 def solution(mesh):

time: 80.8 us -> 74.1 us (0.917)
  local copies, waits for them, and re-layouts: 7.44 us -> 2.19 us
  Pallas kernels: 72.9 us -> 71.6 us
    unnamed x1 -> x0, local copies, waits for them, and re-layouts: 5.26 us -> none
    pallas_call x1, Pallas kernels: 72.9 us -> 71.6 us  [mirrored_sums(): pl.pallas_call(functools.partial(kernel, nz, rows, cols, nmo // nocc, ha)...]
where the time goes in v2:
time: 74.1 us; the launch traced here: 73.8 us
  Pallas kernels  71.6 us (97%)
  local copies, waits for them, and re-layouts  2.19 us (3%)
    pallas_call x1, Pallas kernels, mirrored_sums(): pl.pallas_call(functools.partial(kernel, nz, rows, cols, nmo // nocc, ha)...  71.6 us
    pallas_call x1, local copies, waits for them, and re-layouts, mirrored_sums(): pl.pallas_call(functools.partial(kernel, nz, rows, cols, nmo // nocc, ha)...  2.19 us

profile of v2, /device:TPU:0, one launch (start us, length us, event | category | flops | bytes accessed | tf_op | source)
XLA Modules:
  0.0 73.8 jit_solution(15008430320115674936)
XLA Ops:
  0.0 71.6 %shard_map.28 = f32[1600,50]{1,0:T(8,128)} custom-call(bf16[2,1600,6400]{2,1,0:T(8,128)(2,1)} %b_ref.1, bf16[2,400,1600]{2,1,0:T(8,128)(2,1)} %bitcast.1), custom_call_target="tpu_custom_call" | custom-call | flops 16384000000 | bytes 40960000 | tf_op jit(solution)/shard_map/pallas_call | solution.py:295
  71.6 2.2 %copy.3 = f32[1600,50]{0,1:T(8,128)} copy(f32[1600,50]{1,0:T(8,128)} %shard_map.28) | data formatting | bytes 640000 | tf_op jit(solution)/shard_map/pallas_call | solution.py:295
